TPU v7x, 128 devices: a whole 4x4x4 slice. The times are simulated.
128 devices in a mesh: row: 8 (over y, core), col: 16 (over z, x).
Axes of the slice: x: 4, y: 4, z: 4, core: 2. Of those that a mesh axis runs over, the one named last changes fastest.
Arguments:
- panel: bfloat16 [256, 512, 128], P('row', 'col'), may hold values from -1.296875 to 1.296875
- bases: bfloat16 [256, 1024, 128], P('row', 'col'), may hold values from -0.5 to 0.5
- pivots: float32 [512], P('col'), may hold values from 0.25 to 4
- ranks: int32 [256], P('row'), may hold values from 32 to 128
- pairs: int32 [256, 2], P('row'), may hold values from 0 to 255, as said below
- targets: bfloat16 [256, 1024, 1024], P('row', 'col'), may hold values from -6 to 6
Outputs:
- updated: bfloat16 [256, 1024, 1024], P('row', 'col')
Inputs may be any that keep to these rules, and one draw needn't show every extreme that they name: Row p has column tile j = pairs[p, 1] in [b * 32, (b + 1) * 32) with b = p // 32, and row tile i = pairs[p, 0] with j <= i.
All inputs are finite; a program needn't handle non-finite values.
Results may differ from a plain program's by a relative error of at most 0.0056.
Values may be sent and summed in bfloat16 or wider, within the bound.
A program may use at most 128 MiB of HBM per device.

v0:
```python
import jax
import jax.numpy as jnp
from jax import lax
from jax.sharding import PartitionSpec as P


def sent_together(arrays, axis, dim, along):
    widths = [a.shape[along] for a in arrays]
    both = jnp.concatenate(arrays, axis=along)
    result = lax.all_gather(both, axis, axis=dim, tiled=True)
    return tuple(jnp.split(result, [sum(widths[:k]) for k in range(1, len(widths))], axis=along))


def split_up(value, dim, length):
    lengths = value.shape
    tiles = value.reshape(*lengths[:dim], length, lengths[dim] // length, *lengths[dim + 1 :])
    return jnp.moveaxis(tiles, dim, 0)


def sum_at_owner(value, axis, dim):
    tiles = split_up(value, dim, lax.axis_size(axis))
    arrived = lax.all_to_all(tiles, axis, split_axis=0, concat_axis=0, tiled=True)
    return arrived.sum(axis=0)


def laid_out(tiles, dim):
    lengths = list(tiles.shape[1:])
    lengths[dim] *= tiles.shape[0]
    return jnp.moveaxis(tiles, 0, dim).reshape(lengths)


def from_everyone(value, axis):
    length = lax.axis_size(axis)
    return lax.all_to_all(
        jnp.broadcast_to(value[None], (length, *value.shape)), axis, 0, 0, tiled=True
    )


def gathered_copies(value, axis, dim):
    return laid_out(from_everyone(value, axis), dim)


def shards(panel, bases, pivots, ranks, pairs, targets):
    keep = lax.broadcasted_iota(jnp.int32, (1, 1, panel.shape[2]), 2) < ranks[:, None, None]
    masked = jnp.where(keep, panel, jnp.zeros_like(panel))
    scaled = (masked.astype(jnp.float32) * pivots[None, :, None]).astype(jnp.bfloat16)
    every_scaled, every_panel = sent_together((scaled, masked), "row", 0, 1)
    row_tile = pairs[:, 0]
    col_tile = pairs[:, 1]
    partial_value = jnp.einsum(
        "pwa,pwb->pab",
        every_scaled[row_tile],
        every_panel[col_tile],
        preferred_element_type=jnp.float32,
    )
    shares = sum_at_owner(partial_value, "col", 0).astype(jnp.bfloat16)
    cores_b = gathered_copies(shares, "col", 0)
    every_rows = lax.all_gather(bases, "row", axis=0, tiled=True)
    left = every_rows[row_tile]
    local_col = col_tile - lax.axis_index("row") * bases.shape[0]
    whole_bases = lax.all_gather(bases, "col", axis=1, tiled=True)
    factor = jnp.einsum(
        "pab,pkb->pak", cores_b, whole_bases[local_col], preferred_element_type=jnp.float32
    ).astype(jnp.bfloat16)
    update = jnp.einsum("pka,pac->pkc", left, factor, preferred_element_type=jnp.float32)
    return (targets.astype(jnp.float32) - update).astype(jnp.bfloat16)


def solution(mesh):
    return jax.shard_map(
        shards,
        mesh=mesh,
        in_specs=(
            P("row", "col", None),
            P("row", "col", None),
            P("col"),
            P("row"),
            P("row", None),
            P("row", "col", None),
        ),
        out_specs=P("row", "col", None),
        check_vma=False,
    )
```

profile of v0, /device:TPU:1, one launch (start us, length us, event | category | flops | bytes accessed | tf_op | source)
XLA Modules:
  0.0 183.6 jit_solution(9021132081819208227)
XLA Ops:
  6.5 0.0 all-gather.6.cloned.1.call-start
  6.5 0.7 iota_compare_fusion
  7.3 1.1 multiply_convert_fusion
  8.4 0.9 pad_maximum_fusion
  9.2 0.0 all-gather.6.cloned.1.call-update
  9.2 0.0 all-gather.4.cloned.1.call-start
  9.3 0.7 all-gather.4.cloned.1.call-update
  10.0 0.0 all-gather.8.cloned.1.call-start
  10.0 0.7 all-gather.8.cloned.1.call-update
  10.7 0.8 fusion.8
  11.5 33.6 %all-gather.6.cloned.1.call-done = bf16[256,64,128]{2,1,0:T(8,128)(2,1)} async-done(((bf16[32,64,128]{2,1,0:T(8,128)(2,1)}), bf16[256,64,128]{2,1,0:T(8,128)(2,1)}) %all-gather.6.cloned.1.call-update) | async-done | bytes 4194320 | tf_op jit(solution)/shard_map/all_gather | solution.py:10
  45.2 4.3 %fusion.9 = (bf16[256,32,128]{2,1,0:T(8,128)(2,1)S(1)}, bf16[256,32,128]{2,1,0:T(8,128)(2,1)}) fusion(bf16[256,64,128]{2,1,0:T(8,128)(2,1)} %all-gather.6.cloned.1.call-done), kind=kLoop, calls=%fused_computation.21 | loop fusion | bytes 8388608 | tf_op jit(solution)/shard_map/split | solution.py:11
  49.5 2.2 %gather_fusion.1 = bf16[32,32,128]{2,1,0:T(8,128)(2,1)S(1)} fusion(bf16[256,32,128]{2,1,0:T(8,128)(2,1)} %get-tuple-element.8, s32[1024]{0:T(1024)S(1)} %pad_clamp_fusion.2), kind=kCustom, calls=%fused_computation.1 | custom fusion | bytes 524416 | tf_op jit(solution)/shard_map/gather | solution.py:52
  51.7 0.6 gather_fusion.2
  52.3 0.5 fusion.10
  52.8 34.1 %all_to_all.10 = f32[16,2,128,128]{3,2,1,0:T(8,128)S(1)} all-to-all(f32[16,2,128,128]{3,2,1,0:T(8,128)S(1)} %bitcast.13), channel_id=1, replica_groups=mesh['row'=8,'col'=16] {'col'}, dimensions={0} | all-to-all | bytes 4194304 | tf_op jit(solution)/shard_map/all_to_all | solution.py:22
  86.9 0.1 reduce_sum.9
  87.0 1.2 broadcast_in_dim.14
  88.2 3.7 %all-to-all-start.1 = ((bf16[16,2,128,128]{3,2,1,0:T(8,128)(2,1)}), bf16[16,2,128,128]{3,2,1,0:T(8,128)(2,1)S(1)}, u32[]{:S(2)}, u32[]{:S(2)}) async-start(bf16[16,2,128,128]{3,2,1,0:T(8,128)(2,1)} %broadcast_in_dim.14), calls=%async_computation.1 | async-start | bytes 2097152 | tf_op jit(solution)/shard_map/all_to_all | solution.py:34
  91.9 0.0 all-gather.4.cloned.1.call-done
  91.9 2.8 %gather_fusion = bf16[32,64,128]{2,1,0:T(8,128)(2,1)S(1)} fusion(bf16[256,64,128]{2,1,0:T(8,128)(2,1)} %all-gather.4.cloned.1.call-done, s32[1024]{0:T(1024)S(1)} %pad_clamp_fusion.2), kind=kCustom, calls=%fused_computation | custom fusion | bytes 1048704 | tf_op jit(solution)/shard_map/gather | solution.py:59
  94.8 66.1 %all-gather.8.cloned.1.call-done = bf16[32,1024,128]{2,1,0:T(8,128)(2,1)} async-done(((bf16[32,64,128]{2,1,0:T(8,128)(2,1)}), bf16[32,1024,128]{2,1,0:T(8,128)(2,1)}) %all-gather.8.cloned.1.call-update) | async-done | bytes 8388624 | tf_op jit(solution)/shard_map/all_gather | solution.py:61
  160.9 8.4 %gather_fusion.3 = bf16[32,1024,128]{2,1,0:T(8,128)(2,1)} fusion(bf16[32,1024,128]{2,1,0:T(8,128)(2,1)} %all-gather.8.cloned.1.call-done, s32[1024]{0:T(1024)S(1)} %pad_clamp_fusion), kind=kCustom, calls=%fused_computation.3 | custom fusion | bytes 16777344 | tf_op jit(solution)/shard_map/gather | solution.py:63
  169.3 0.0 all-to-all-done.1
  169.3 7.8 %subtract_convert_fusion = bf16[32,64,1024]{2,1,0:T(8,128)(2,1)} fusion(bf16[32,64,1024]{2,1,0:T(8,128)(2,1)} %param.11, bf16[32,64,128]{2,1,0:T(8,128)(2,1)S(1)} %gather_fusion, bf16[32,128,128]{2,1,0:T(8,128)(2,1)S(1)} %bitcast.14, bf16[32,1024,128]{2,1,0:T(8,128)(2,1)} %gather_fusion.3), kind=kOutput, calls=%fused_computation.4 | convolution fusion | flops 1621098496 | bytes 18350080 | tf_op jit(solution)/shard_map/pka,pac->pkc/dot_general | solution.py:65
  (3 shorter events, 0.0 us)
Async XLA Ops:
  6.5 38.6 %all-gather.6.cloned.1.call-start = ((), (), s32[]{:S(2)}) async-start(), calls=%async_computation.3 | async-start | bytes 4718592 | tf_op jit(solution)/shard_map/all_gather | solution.py:10
  9.2 82.7 %all-gather.4.cloned.1.call-start = ((), (), s32[]{:S(2)}) async-start(), calls=%async_computation.2 | async-start | bytes 4718592 | tf_op jit(solution)/shard_map/all_gather | solution.py:58
  10.0 150.9 %all-gather.8.cloned.1.call-start = ((), (), s32[]{:S(2)}) async-start(), calls=%async_computation.4 | async-start | bytes 8912896 | tf_op jit(solution)/shard_map/all_gather | solution.py:61
  88.2 81.0 %all-to-all-start.1 = ((bf16[16,2,128,128]{3,2,1,0:T(8,128)(2,1)}), bf16[16,2,128,128]{3,2,1,0:T(8,128)(2,1)S(1)}, u32[]{:S(2)}, u32[]{:S(2)}) async-start(bf16[16,2,128,128]{3,2,1,0:T(8,128)(2,1)} %broadcast_in_dim.14), calls=%async_computation.1 | async-start | bytes 2097152 | tf_op jit(solution)/shard_map/all_to_all | solution.py:34
Sparse Core Ops, SparseCore 0:
  9.4 35.7 all-gather.5
  46.9 32.0 all-gather.3
  81.1 79.6 all-gather.7
where the time goes:
time: 184 us
  waiting for transfers between devices  101 us (55%)
  blocking collectives  34.1 us (19%)
  local copies, waits for them, and re-layouts  19.5 us (11%)
  between operations  13.2 us (7%)
  matrix products  8.31 us (5%)
  starting transfers between devices  3.75 us (2%)
  other arithmetic  3.55 us (2%)
    all_gather x1, waiting for transfers between devices, shards(): whole_bases = lax.all_gather(bases, 'col', axis=1, tiled=True)  66.1 us
    all_to_all x1, blocking collectives, sum_at_owner(): lax.all_to_all(tiles, axis, split_axis=0, concat_axis=0, tiled=True)  34.1 us
    all_gather x1, waiting for transfers between devices, sent_together(): result = lax.all_gather(both, axis, axis=dim, tiled=True)  33.6 us
    gather x1, local copies, waits for them, and re-layouts, shards(): whole_bases[local_col]  8.4 us
    dot_general x1, matrix products, shards(): jnp.einsum('pka,pac->pkc', left, factor, preferred_element_type=jnp.float32)  7.82 us
    split x1, local copies, waits for them, and re-layouts, sent_together(): jnp.split(result, [sum(widths[:k]) for k in range(1, len(widths))], axis=...  4.31 us
  transfers between devices with their start and end apart: 4, of which 2 were waited for; matrix products, arithmetic and copies ran while one was open for 11% of the time, Pallas kernels for 0%

commit v1 on v0

v1 whole, which is shorter than its diff:
```python
import jax
import jax.numpy as jnp
from jax import lax
from jax.experimental import pallas as pl
from jax.experimental.pallas import tpu as pltpu
from jax.sharding import PartitionSpec as P

MESH = pl.DeviceIdType.MESH
F32 = jnp.float32
BF16 = jnp.bfloat16
SIDE = 4


def wrap(v):
    return lax.rem(v + 2 * SIDE, SIDE)


def near(d):
    return (d + 1) % SIDE - 1


def kernel(
    panel, bases, pivots, ranks, pairs, targets, out,
    here, above, below, across, lefts, tiles, mine, ready, transit, operands, cores, lead, held, scale,
    send_sem, recv_sem, local_sem,
):
    row = lax.axis_index("row")
    col = lax.axis_index("col")
    y, core = lax.div(row, 2), lax.rem(row, 2)
    z, x = lax.div(col, SIDE), lax.rem(col, SIDE)
    n_tiles, depth, rank = panel.shape
    part = bases.shape[1]
    half = n_tiles // 2
    n_pairs = held.shape[0]
    whole = {0: here, 1: above, -1: below, 2: across}

    def at_col(dz, dx):
        return (row, wrap(z + dz) * SIDE + wrap(x + dx))

    def at_row(dy):
        return (wrap(y + dy) * 2 + core, col)

    twin = (y * 2 + 1 - core, col)

    kept = []

    def move(src, dst):
        copy = pltpu.make_async_copy(src, dst, local_sem.at[len(kept)])
        copy.start()
        kept.append(copy)
        return copy

    own_tiles = pl.ds(row * n_tiles, n_tiles)
    get_panel = move(panel, mine)
    get_here = move(bases, here.at[x])
    get_left = move(bases, lefts.at[own_tiles])
    get_targets = move(targets, held)

    barrier = pltpu.get_barrier_semaphore()
    friends = [at_col(0, 1), at_col(0, -1), at_col(1, 0), at_col(-1, 0), at_row(1), at_row(-1), twin]
    friends += [at_col(0, 2), at_col(2, 0)]
    for friend in friends:
        pl.semaphore_signal(barrier, inc=1, device_id=friend, device_id_type=MESH)
    for r in range(depth):
        scale[pl.ds(r, 1), :] = jnp.full((1, rank), pivots[r], F32)
    pl.semaphore_wait(barrier, len(friends))

    sent = []

    def send(src, dst, to):
        k = len(sent)
        copy = pltpu.make_async_remote_copy(
            src_ref=src,
            dst_ref=dst,
            send_sem=send_sem.at[k],
            recv_sem=recv_sem.at[k],
            device_id=to,
            device_id_type=MESH,
        )
        copy.start()
        sent.append(copy)
        return copy

    def pass_on(dz, at_x, to, first, count, fresh=False):
        some = pl.ds(first, count)
        src = bases.at[some] if fresh else whole[near(dz)].at[at_x, some]
        return send(src, whole[near(dz - to[0])].at[at_x, some], at_col(*to))

    def along_x(dz, first, fresh=False):
        return [pass_on(dz, x, (0, d), first, half, fresh) for d in (1, -1)]

    def along_x_far(dz, first, arriving):
        quarter = half // 2
        arriving[0].wait_recv()
        a = pass_on(dz, wrap(x - 1), (0, 1), first, quarter)
        arriving[1].wait_recv()
        b = pass_on(dz, wrap(x + 1), (0, -1), first + quarter, quarter)
        return [a, b]

    def along_z(dx, first, fresh=False):
        return [pass_on(0, wrap(x + dx), (d, 0), first, half, fresh) for d in (1, -1)]

    def along_z_far(dx, first, arriving):
        quarter = half // 2
        arriving[0].wait_recv()
        a = pass_on(-1, wrap(x + dx), (1, 0), first, quarter)
        arriving[1].wait_recv()
        b = pass_on(1, wrap(x + dx), (-1, 0), first + quarter, quarter)
        return [a, b]

    def own_row(array):
        block = array.at[own_tiles]
        return [send(block, block, to) for to in (at_row(1), at_row(-1), twin)]

    def far_row(array, arriving):
        got = []
        for k, d in ((0, -1), (1, 1)):
            first = (wrap(y + d) * 2 + core) * n_tiles
            arriving[k].wait_recv()
            block = array.at[pl.ds(first + k * half, half)]
            got.append(send(block, block, at_row(-d)))
            block = array.at[pl.ds(first, n_tiles)]
            got.append(send(block, block, twin))
        return got

    def last_row(array, arriving):
        first = (wrap(y + 2) * 2 + core) * n_tiles
        got = []
        for k in (0, 1):
            arriving[2 * k].wait_recv()
            block = array.at[pl.ds(first + k * half, half)]
            got.append(send(block, block, twin))
        return got

    def wait_all(copies):
        for copy in copies:
            copy.wait_recv()

    far_x, far_z, first_z, first_x = {}, {}, {}, {}
    in_x = along_x(0, 0, True)
    in_z = along_z(0, half, True)
    first_z[0] = along_z(0, 0, True)
    first_x[0] = along_x(0, half, True)

    get_panel.wait()
    lanes = lax.broadcasted_iota(jnp.int32, (depth, rank), 1)

    @pl.loop(0, n_tiles)
    def _(t):
        tile = mine[t].astype(F32)
        tiles[row * n_tiles + t] = jnp.where(lanes < ranks[t], tile, jnp.zeros_like(tile)).astype(BF16)

    panel_in = own_row(tiles)
    panel_far = far_row(tiles, panel_in)
    get_left.wait()
    left_in = own_row(lefts)
    panel_last = last_row(tiles, panel_far)
    wait_all([panel_in[2], panel_far[1], panel_far[3], *panel_last])

    @pl.loop(0, n_pairs)
    def _(p):
        to = lax.div(p, 2)
        pr, tz, tx = lax.rem(p, 2), lax.div(to, SIDE), lax.rem(to, SIDE)
        scaled = (tiles[pairs[p, 0]].astype(F32) * scale[...]).astype(BF16)
        ready[tx, tz, 0, pr] = scaled
        ready[tx, tz, 1, pr] = tiles[pairs[p, 1]]

    own_transit = move(ready.at[x], transit.at[:, :, :, x])
    stage_x = [
        send(ready.at[wrap(x + d)], transit.at[:, :, :, x], at_col(0, d)) for d in (1, -1, 2)
    ]

    far_x[0] = along_x_far(0, 0, in_x)
    far_z[0] = along_z_far(0, half, in_z)
    for d in (-1, 1):
        first_z[d] = along_z(d, 0)
        first_x[d] = along_x(d, half)
    left_far = far_row(lefts, left_in)

    own_transit.wait()
    wait_all(stage_x)
    mid = pl.ds(z * SIDE, SIDE)
    own_operands = move(transit.at[z], operands.at[:, :, mid])
    stage_z = [
        send(transit.at[wrap(z + d)], operands.at[:, :, mid], at_col(d, 0)) for d in (1, -1, 2)
    ]

    late_z = {0: along_z_far(0, 0, first_z[0])}
    late_x = {0: along_x_far(0, half, first_x[0])}
    wait_all(far_x[0] + far_z[0])
    first_z[2] = along_z(2, 0)
    first_x[2] = along_x(2, half)
    left_last = last_row(lefts, left_far)

    own_operands.wait()
    wait_all(stage_z)
    for pr in (0, 1):
        a = operands[0, pr].reshape(SIDE * SIDE * depth, rank)
        b = operands[1, pr].reshape(SIDE * SIDE * depth, rank)
        total = lax.dot_general(a, b, (((0,), (0,)), ((), ())), preferred_element_type=F32)
        cores[z, x, pr] = total.astype(BF16)
    mine_0, mine_1 = cores.at[z, x, 0], cores.at[z, x, 1]
    core_x = [send(mine_0, mine_0, at_col(0, d)) for d in (1, -1, 2)]
    core_z = [send(mine_1, mine_1, at_col(d, 0)) for d in (1, -1, 2)]

    for d in (-1, 1):
        late_z[d] = along_z_far(d, 0, first_z[d])
        late_x[d] = along_x_far(d, half, first_x[d])

    wait_all(core_x)
    line = cores.at[z, :, 0]
    core_last = [send(line, line, at_col(d, 0)) for d in (1, -1, 2)]
    wait_all(core_z)
    line = cores.at[:, x, 1]
    core_last += [send(line, line, at_col(0, d)) for d in (1, -1, 2)]

    late_z[2] = along_z_far(2, 0, first_z[2])
    late_x[2] = along_x_far(2, half, first_x[2])

    wait_all([left_in[2], left_far[1], left_far[3], *left_last, *core_last])

    @pl.loop(0, n_pairs)
    def _(p):
        to = lax.div(p, 2)
        pr, tz, tx = lax.rem(p, 2), lax.div(to, SIDE), lax.rem(to, SIDE)
        product = jnp.dot(lefts[pairs[p, 0]], cores[tz, tx, pr], preferred_element_type=F32)
        lead[p] = product.astype(BF16)

    width = SIDE * part
    get_here.wait()
    get_targets.wait()
    done = []

    def update(dz):
        group = whole[dz]
        columns = pl.ds(pl.multiple_of(wrap(z + dz) * width, width), width)

        @pl.loop(0, n_pairs)
        def _(p):
            right = group[:, lax.rem(pairs[p, 1], n_tiles)].reshape(width, rank)
            change = lax.dot_general(
                lead[p], right, (((1,), (1,)), ((), ())), preferred_element_type=F32
            )
            held[p, :, columns] = (held[p, :, columns].astype(F32) - change).astype(BF16)

        done.append(move(held.at[:, :, columns], out.at[:, :, columns]))

    wait_all(late_x[0])
    update(0)
    wait_all(late_x[1] + late_x[-1])
    update(1)
    update(-1)
    wait_all(late_x[2] + [c for d in (0, -1, 1, 2) for c in late_z[d]])
    update(2)
    for copy in done:
        copy.wait()
    for copy in sent:
        copy.wait_send()


def shards(panel, bases, pivots, ranks, pairs, targets):
    n_tiles, depth, rank = panel.shape
    part = bases.shape[1]
    n_pairs = pairs.shape[0]
    n_rows = lax.axis_size("row")
    group = pltpu.VMEM((SIDE, n_tiles, part, rank), BF16)
    smem = pl.BlockSpec(memory_space=pltpu.SMEM)
    hbm = pl.BlockSpec(memory_space=pl.ANY)
    return pl.pallas_call(
        kernel,
        out_shape=jax.ShapeDtypeStruct(targets.shape, targets.dtype),
        in_specs=[hbm, hbm, smem, smem, smem, hbm],
        out_specs=hbm,
        scratch_shapes=[
            group,
            group,
            group,
            group,
            pltpu.VMEM((n_rows * n_tiles, part, rank), BF16),
            pltpu.VMEM((n_rows * n_tiles, depth, rank), BF16),
            pltpu.VMEM((n_tiles, depth, rank), BF16),
            pltpu.VMEM((SIDE, SIDE, 2, 2, depth, rank), BF16),
            pltpu.VMEM((SIDE, 2, 2, SIDE, depth, rank), BF16),
            pltpu.VMEM((2, 2, SIDE * SIDE, depth, rank), BF16),
            pltpu.VMEM((SIDE, SIDE, 2, rank, rank), BF16),
            pltpu.VMEM((n_pairs, part, rank), BF16),
            pltpu.VMEM(targets.shape, BF16),
            pltpu.VMEM((depth, rank), F32),
            pltpu.SemaphoreType.DMA((80,)),
            pltpu.SemaphoreType.DMA((80,)),
            pltpu.SemaphoreType.DMA((12,)),
        ],
        compiler_params=pltpu.CompilerParams(
            collective_id=0, has_side_effects=True, vmem_limit_bytes=48 << 20
        ),
    )(panel, bases, pivots, ranks, pairs, targets)


def solution(mesh):
    return jax.shard_map(
        shards,
        mesh=mesh,
        in_specs=(
            P("row", "col", None),
            P("row", "col", None),
            P("col"),
            P("row"),
            P("row", None),
            P("row", "col", None),
        ),
        out_specs=P("row", "col", None),
        check_vma=False,
    )
```

time: 184 us -> 100 us (0.54)
  waiting for transfers between devices: 101 us -> 0 us
  Pallas kernels: 0 us -> 94.1 us
  blocking collectives: 34.1 us -> 0 us
  local copies, waits for them, and re-layouts: 19.5 us -> 6.07 us
  between operations: 13.2 us -> 0.01 us
  matrix products: 8.31 us -> 0 us
  starting transfers between devices: 3.75 us -> 0 us
  other arithmetic: 3.55 us -> 0 us
    all_gather x3 -> x0, waiting for transfers between devices: 99.7 us -> none  [the longest x1 66.1 us: shards(): whole_bases = lax.all_gather(bases, 'col', axis=1, tiled=True)]
    pallas_call x0 -> x1, Pallas kernels: none -> 94.1 us  [shards(): pl.pallas_call(kernel, out_shape=jax.ShapeDtypeStruct(targets.shape, targ...]
    all_to_all x1 -> x0, blocking collectives: 34.1 us -> none  [sum_at_owner(): lax.all_to_all(tiles, axis, split_axis=0, concat_axis=0, tiled=True)]
    gather x4 -> x0, local copies, waits for them, and re-layouts: 14 us -> none  [the longest x1 8.4 us: shards(): whole_bases[local_col]]
    dot_general x2 -> x0, matrix products: 8.31 us -> none  [the longest x1 7.82 us: shards(): jnp.einsum('pka,pac->pkc', left, factor, preferred_element_type=jnp.float32)]
    unnamed x0 -> x10, local copies, waits for them, and re-layouts: none -> 6.07 us
    split x1 -> x0, local copies, waits for them, and re-layouts: 4.31 us -> none  [sent_together(): jnp.split(result, [sum(widths[:k]) for k in range(1, len(widths))], axis=...]
    all_to_all x1 -> x0, starting transfers between devices: 3.67 us -> none  [from_everyone(): lax.all_to_all(jnp.broadcast_to(value[None], (length, *value.shape)), axi...]
  transfers between devices with their start and end apart: 4 -> 0, of which waited for: 2 -> 0; matrix products, arithmetic and copies ran while one was open for 11% -> 0% of each run, Pallas kernels for 0% -> 0%
where the time goes in v1:
time: 100 us
  Pallas kernels  94.1 us (94%)
  local copies, waits for them, and re-layouts  6.07 us (6%)
    pallas_call x1, Pallas kernels, shards(): pl.pallas_call(kernel, out_shape=jax.ShapeDtypeStruct(targets.shape, targ...  94.1 us
    unnamed x10, local copies, waits for them, and re-layouts  6.07 us

profile of v1, /device:TPU:1, one launch (start us, length us, event | category | flops | bytes accessed | tf_op | source)
XLA Modules:
  0.0 100.1 jit_solution(1167948985013436064)
XLA Ops:
  0.0 0.8 copy.7.pairs
  0.8 0.0 copy-start
  0.8 1.0 %copy-done = bf16[32,64,128]{2,1,0:T(8,128)(2,1)S(1)} copy-done((bf16[32,64,128]{2,1,0:T(8,128)(2,1)S(1)}, bf16[32,64,128]{2,1,0:T(8,128)(2,1)}, u32[]{:S(2)}) %copy-start) | copy-done | bytes 524312
  1.8 0.0 copy-start.1
  1.8 0.9 copy-done.1
  2.8 0.0 copy-start.2
  2.8 0.7 copy-done.2
  3.4 0.0 copy-start.3
  3.4 0.7 copy-done.3
  4.1 94.1 %shard_map.64 = bf16[32,64,1024]{2,1,0:T(8,128)(2,1)S(1)} custom-call(bf16[32,32,128]{2,1,0:T(8,128)(2,1)S(1)} %copy-done.1, bf16[32,64,128]{2,1,0:T(8,128)(2,1)S(1)} %copy-done, f32[32]{0:T(128)S(1)} %copy-done.2, s32[32]{0:T(128)S(1)} %copy-done.3, s32[32,2]{1,0:T(8,128)S(1)} %copy.7.pairs, bf16[32,64,1024]{2,1,0:T(8,128)(2,1)} %targets.1), custom_call_target="tpu_custom_call" | custom-call | tf_op jit(solution)/shard_map/pallas_call | solution.py:269
  98.1 2.0 %copy.9 = bf16[32,64,1024]{2,1,0:T(8,128)(2,1)} copy(bf16[32,64,1024]{2,1,0:T(8,128)(2,1)S(1)} %shard_map.64) | data formatting | bytes 8388608
Async XLA Ops:
  0.8 1.0 %copy-start = (bf16[32,64,128]{2,1,0:T(8,128)(2,1)S(1)}, bf16[32,64,128]{2,1,0:T(8,128)(2,1)}, u32[]{:S(2)}) copy-start(bf16[32,64,128]{2,1,0:T(8,128)(2,1)} %bases.1) | copy-start | bytes 1572868
  1.8 0.9 copy-start.1
  2.8 0.7 copy-start.2
  3.4 0.7 copy-start.3

commit v2 on v1

--- a/solution.py
+++ b/solution.py
@@ -20,8 +20,8 @@
 
 
 def kernel(
-    panel, bases, pivots, ranks, pairs, targets, out,
-    here, above, below, across, lefts, tiles, mine, ready, transit, operands, cores, lead, held, scale,
+    panel, bases, pivot_list, rank_list, pair_list, targets, out,
+    pivots, ranks, pairs, here, above, below, across, lefts, tiles, mine, ready, transit, operands, cores, lead, scale,
     send_sem, recv_sem, local_sem,
 ):
     row = lax.axis_index("row")
@@ -31,7 +31,7 @@
     n_tiles, depth, rank = panel.shape
     part = bases.shape[1]
     half = n_tiles // 2
-    n_pairs = held.shape[0]
+    n_pairs = out.shape[0]
     whole = {0: here, 1: above, -1: below, 2: across}
 
     def at_col(dz, dx):
@@ -51,18 +51,33 @@
         return copy
 
     own_tiles = pl.ds(row * n_tiles, n_tiles)
+    get_ranks = move(rank_list, ranks)
     get_panel = move(panel, mine)
+    get_pivots = move(pivot_list, pivots)
+    get_pairs = move(pair_list, pairs)
     get_here = move(bases, here.at[x])
     get_left = move(bases, lefts.at[own_tiles])
-    get_targets = move(targets, held)
+    get_targets = move(targets, out)
 
     barrier = pltpu.get_barrier_semaphore()
     friends = [at_col(0, 1), at_col(0, -1), at_col(1, 0), at_col(-1, 0), at_row(1), at_row(-1), twin]
     friends += [at_col(0, 2), at_col(2, 0)]
     for friend in friends:
         pl.semaphore_signal(barrier, inc=1, device_id=friend, device_id_type=MESH)
+
+    get_ranks.wait()
+    get_panel.wait()
+    lanes = lax.broadcasted_iota(jnp.int32, (depth, rank), 1)
+
+    @pl.loop(0, n_tiles, unroll=4)
+    def _(t):
+        tile = mine[t].astype(F32)
+        tiles[row * n_tiles + t] = jnp.where(lanes < ranks[t], tile, jnp.zeros_like(tile)).astype(BF16)
+
+    get_pivots.wait()
     for r in range(depth):
         scale[pl.ds(r, 1), :] = jnp.full((1, rank), pivots[r], F32)
+    get_pairs.wait()
     pl.semaphore_wait(barrier, len(friends))
 
     sent = []
@@ -136,46 +151,36 @@
         for copy in copies:
             copy.wait_recv()
 
-    far_x, far_z, first_z, first_x = {}, {}, {}, {}
+    far_x, far_z, first_z, first_x, late_z, late_x = {}, {}, {}, {}, {}, {}
     in_x = along_x(0, 0, True)
     in_z = along_z(0, half, True)
+    panel_in = own_row(tiles)
     first_z[0] = along_z(0, 0, True)
     first_x[0] = along_x(0, half, True)
-
-    get_panel.wait()
-    lanes = lax.broadcasted_iota(jnp.int32, (depth, rank), 1)
-
-    @pl.loop(0, n_tiles)
-    def _(t):
-        tile = mine[t].astype(F32)
-        tiles[row * n_tiles + t] = jnp.where(lanes < ranks[t], tile, jnp.zeros_like(tile)).astype(BF16)
-
-    panel_in = own_row(tiles)
     panel_far = far_row(tiles, panel_in)
+    far_x[0] = along_x_far(0, 0, in_x)
+    far_z[0] = along_z_far(0, half, in_z)
     get_left.wait()
     left_in = own_row(lefts)
     panel_last = last_row(tiles, panel_far)
     wait_all([panel_in[2], panel_far[1], panel_far[3], *panel_last])
 
-    @pl.loop(0, n_pairs)
+    @pl.loop(0, n_pairs, unroll=4)
     def _(p):
         to = lax.div(p, 2)
         pr, tz, tx = lax.rem(p, 2), lax.div(to, SIDE), lax.rem(to, SIDE)
-        scaled = (tiles[pairs[p, 0]].astype(F32) * scale[...]).astype(BF16)
+        scaled = (tiles[pairs[0, p]].astype(F32) * scale[...]).astype(BF16)
         ready[tx, tz, 0, pr] = scaled
-        ready[tx, tz, 1, pr] = tiles[pairs[p, 1]]
+        ready[tx, tz, 1, pr] = tiles[pairs[1, p]]
 
     own_transit = move(ready.at[x], transit.at[:, :, :, x])
     stage_x = [
         send(ready.at[wrap(x + d)], transit.at[:, :, :, x], at_col(0, d)) for d in (1, -1, 2)
     ]
 
-    far_x[0] = along_x_far(0, 0, in_x)
-    far_z[0] = along_z_far(0, half, in_z)
-    for d in (-1, 1):
-        first_z[d] = along_z(d, 0)
-        first_x[d] = along_x(d, half)
-    left_far = far_row(lefts, left_in)
+    first_z[1] = along_z(1, 0)
+    first_x[1] = along_x(1, half)
+    late_z[0] = along_z_far(0, 0, first_z[0])
 
     own_transit.wait()
     wait_all(stage_x)
@@ -185,12 +190,10 @@
         send(transit.at[wrap(z + d)], operands.at[:, :, mid], at_col(d, 0)) for d in (1, -1, 2)
     ]
 
-    late_z = {0: along_z_far(0, 0, first_z[0])}
-    late_x = {0: along_x_far(0, half, first_x[0])}
-    wait_all(far_x[0] + far_z[0])
-    first_z[2] = along_z(2, 0)
-    first_x[2] = along_x(2, half)
-    left_last = last_row(lefts, left_far)
+    late_x[0] = along_x_far(0, half, first_x[0])
+    first_x[-1] = along_x(-1, half)
+    first_z[-1] = along_z(-1, 0)
+    left_far = far_row(lefts, left_in)
 
     own_operands.wait()
     wait_all(stage_z)
@@ -203,9 +206,10 @@
     core_x = [send(mine_0, mine_0, at_col(0, d)) for d in (1, -1, 2)]
     core_z = [send(mine_1, mine_1, at_col(d, 0)) for d in (1, -1, 2)]
 
-    for d in (-1, 1):
-        late_z[d] = along_z_far(d, 0, first_z[d])
-        late_x[d] = along_x_far(d, half, first_x[d])
+    wait_all(far_x[0] + far_z[0])
+    first_z[2] = along_z(2, 0)
+    first_x[2] = along_x(2, half)
+    left_last = last_row(lefts, left_far)
 
     wait_all(core_x)
     line = cores.at[z, :, 0]
@@ -214,36 +218,34 @@
     line = cores.at[:, x, 1]
     core_last += [send(line, line, at_col(0, d)) for d in (1, -1, 2)]
 
-    late_z[2] = along_z_far(2, 0, first_z[2])
-    late_x[2] = along_x_far(2, half, first_x[2])
+    for d in (-1, 1, 2):
+        late_z[d] = along_z_far(d, 0, first_z[d])
+        late_x[d] = along_x_far(d, half, first_x[d])
 
     wait_all([left_in[2], left_far[1], left_far[3], *left_last, *core_last])
 
-    @pl.loop(0, n_pairs)
+    @pl.loop(0, n_pairs, unroll=4)
     def _(p):
         to = lax.div(p, 2)
         pr, tz, tx = lax.rem(p, 2), lax.div(to, SIDE), lax.rem(to, SIDE)
-        product = jnp.dot(lefts[pairs[p, 0]], cores[tz, tx, pr], preferred_element_type=F32)
+        product = jnp.dot(lefts[pairs[0, p]], cores[tz, tx, pr], preferred_element_type=F32)
         lead[p] = product.astype(BF16)
 
     width = SIDE * part
     get_here.wait()
     get_targets.wait()
-    done = []
 
     def update(dz):
         group = whole[dz]
         columns = pl.ds(pl.multiple_of(wrap(z + dz) * width, width), width)
 
-        @pl.loop(0, n_pairs)
+        @pl.loop(0, n_pairs, unroll=8)
         def _(p):
-            right = group[:, lax.rem(pairs[p, 1], n_tiles)].reshape(width, rank)
+            right = group[:, lax.rem(pairs[1, p], n_tiles)].reshape(width, rank)
             change = lax.dot_general(
                 lead[p], right, (((1,), (1,)), ((), ())), preferred_element_type=F32
             )
-            held[p, :, columns] = (held[p, :, columns].astype(F32) - change).astype(BF16)
-
-        done.append(move(held.at[:, :, columns], out.at[:, :, columns]))
+            out[p, :, columns] = (out[p, :, columns].astype(F32) - change).astype(BF16)
 
     wait_all(late_x[0])
     update(0)
@@ -252,8 +254,6 @@
     update(-1)
     wait_all(late_x[2] + [c for d in (0, -1, 1, 2) for c in late_z[d]])
     update(2)
-    for copy in done:
-        copy.wait()
     for copy in sent:
         copy.wait_send()
 
@@ -264,14 +264,16 @@
     n_pairs = pairs.shape[0]
     n_rows = lax.axis_size("row")
     group = pltpu.VMEM((SIDE, n_tiles, part, rank), BF16)
-    smem = pl.BlockSpec(memory_space=pltpu.SMEM)
-    hbm = pl.BlockSpec(memory_space=pl.ANY)
+    hbm = pl.BlockSpec(memory_space=pltpu.HBM)
     return pl.pallas_call(
         kernel,
         out_shape=jax.ShapeDtypeStruct(targets.shape, targets.dtype),
-        in_specs=[hbm, hbm, smem, smem, smem, hbm],
-        out_specs=hbm,
+        in_specs=[hbm] * 6,
+        out_specs=pl.BlockSpec(memory_space=pltpu.VMEM),
         scratch_shapes=[
+            pltpu.SMEM(pivots.shape, F32),
+            pltpu.SMEM(ranks.shape, jnp.int32),
+            pltpu.SMEM((2, n_pairs), jnp.int32),
             group,
             group,
             group,
@@ -284,7 +286,6 @@
             pltpu.VMEM((2, 2, SIDE * SIDE, depth, rank), BF16),
             pltpu.VMEM((SIDE, SIDE, 2, rank, rank), BF16),
             pltpu.VMEM((n_pairs, part, rank), BF16),
-            pltpu.VMEM(targets.shape, BF16),
             pltpu.VMEM((depth, rank), F32),
             pltpu.SemaphoreType.DMA((80,)),
             pltpu.SemaphoreType.DMA((80,)),
@@ -293,7 +294,7 @@
         compiler_params=pltpu.CompilerParams(
             collective_id=0, has_side_effects=True, vmem_limit_bytes=48 << 20
         ),
-    )(panel, bases, pivots, ranks, pairs, targets)
+    )(*(pltpu.with_memory_space_constraint(a, pltpu.HBM) for a in (panel, bases, pivots, ranks, pairs.T, targets)))
 
 
 def solution(mesh):

time: 100 us -> 70.2 us (0.70)
  Pallas kernels: 94.1 us -> 68.1 us
  local copies, waits for them, and re-layouts: 6.07 us -> 2.02 us
    pallas_call x1, Pallas kernels: 94.1 us -> 68.1 us  [shards(): pl.pallas_call(kernel, out_shape=jax.ShapeDtypeStruct(targets.shape, targ...]
    unnamed x10 -> x1, local copies, waits for them, and re-layouts: 6.07 us -> 2.02 us
where the time goes in v2:
time: 70.2 us; the launch traced here: 70.1 us
  Pallas kernels  68.1 us (97%)
  local copies, waits for them, and re-layouts  2.02 us (3%)
    pallas_call x1, Pallas kernels, shards(): pl.pallas_call(kernel, out_shape=jax.ShapeDtypeStruct(targets.shape, targ...  68.1 us
    unnamed x1, local copies, waits for them, and re-layouts  2.02 us

profile of v2, /device:TPU:1, one launch (start us, length us, event | category | flops | bytes accessed | tf_op | source)
XLA Modules:
  0.0 70.1 jit_solution(7689063307842927615)
XLA Ops:
  0.0 68.1 %shard_map.64 = bf16[32,64,1024]{2,1,0:T(8,128)(2,1)S(1)} custom-call(bf16[32,32,128]{2,1,0:T(8,128)(2,1)} %panel.1, bf16[32,64,128]{2,1,0:T(8,128)(2,1)} %bases.1, f32[32]{0:T(128)} %pivot_list.1, s32[32]{0:T(128)} %rank_list.1, s32[2,32]{1,0:T(2,128)} %bitcast.1, bf16[32,64,1024]{2,1,0:T(8,128)(2,1)} %targets.1), custom_call_target="tpu_custom_call" | custom-call | tf_op jit(solution)/shard_map/pallas_call | solution.py:268
  68.1 2.0 %copy.8 = bf16[32,64,1024]{2,1,0:T(8,128)(2,1)} copy(bf16[32,64,1024]{2,1,0:T(8,128)(2,1)S(1)} %shard_map.64) | data formatting | bytes 8388608

commit v3 on v2

--- a/solution.py
+++ b/solution.py
@@ -21,7 +21,7 @@
 
 def kernel(
     panel, bases, pivot_list, rank_list, pair_list, targets, out,
-    pivots, ranks, pairs, here, above, below, across, lefts, tiles, mine, ready, transit, operands, cores, lead, scale,
+    pivots, ranks, pairs, here, above, below, across, lefts, tiles, mine, ready, transit, partial, arrived, cores, lead, scale,
     send_sem, recv_sem, local_sem,
 ):
     row = lax.axis_index("row")
@@ -42,6 +42,12 @@
 
     twin = (y * 2 + 1 - core, col)
 
+    barrier = pltpu.get_barrier_semaphore()
+    friends = [at_col(0, 1), at_col(0, -1), at_col(1, 0), at_col(-1, 0), at_row(1), at_row(-1), twin]
+    friends += [at_col(0, 2), at_col(2, 0)]
+    for friend in friends:
+        pl.semaphore_signal(barrier, inc=1, device_id=friend, device_id_type=MESH)
+
     kept = []
 
     def move(src, dst):
@@ -59,25 +65,6 @@
     get_left = move(bases, lefts.at[own_tiles])
     get_targets = move(targets, out)
 
-    barrier = pltpu.get_barrier_semaphore()
-    friends = [at_col(0, 1), at_col(0, -1), at_col(1, 0), at_col(-1, 0), at_row(1), at_row(-1), twin]
-    friends += [at_col(0, 2), at_col(2, 0)]
-    for friend in friends:
-        pl.semaphore_signal(barrier, inc=1, device_id=friend, device_id_type=MESH)
-
-    get_ranks.wait()
-    get_panel.wait()
-    lanes = lax.broadcasted_iota(jnp.int32, (depth, rank), 1)
-
-    @pl.loop(0, n_tiles, unroll=4)
-    def _(t):
-        tile = mine[t].astype(F32)
-        tiles[row * n_tiles + t] = jnp.where(lanes < ranks[t], tile, jnp.zeros_like(tile)).astype(BF16)
-
-    get_pivots.wait()
-    for r in range(depth):
-        scale[pl.ds(r, 1), :] = jnp.full((1, rank), pivots[r], F32)
-    get_pairs.wait()
     pl.semaphore_wait(barrier, len(friends))
 
     sent = []
@@ -101,8 +88,8 @@
         src = bases.at[some] if fresh else whole[near(dz)].at[at_x, some]
         return send(src, whole[near(dz - to[0])].at[at_x, some], at_col(*to))
 
-    def along_x(dz, first, fresh=False):
-        return [pass_on(dz, x, (0, d), first, half, fresh) for d in (1, -1)]
+    def along_x(dz, first, fresh=False, count=half):
+        return [pass_on(dz, x, (0, d), first, count, fresh) for d in (1, -1)]
 
     def along_x_far(dz, first, arriving):
         quarter = half // 2
@@ -112,8 +99,8 @@
         b = pass_on(dz, wrap(x + 1), (0, -1), first + quarter, quarter)
         return [a, b]
 
-    def along_z(dx, first, fresh=False):
-        return [pass_on(0, wrap(x + dx), (d, 0), first, half, fresh) for d in (1, -1)]
+    def along_z(dx, first, fresh=False, count=half):
+        return [pass_on(0, wrap(x + dx), (d, 0), first, count, fresh) for d in (1, -1)]
 
     def along_z_far(dx, first, arriving):
         quarter = half // 2
@@ -154,75 +141,118 @@
     far_x, far_z, first_z, first_x, late_z, late_x = {}, {}, {}, {}, {}, {}
     in_x = along_x(0, 0, True)
     in_z = along_z(0, half, True)
-    panel_in = own_row(tiles)
     first_z[0] = along_z(0, 0, True)
     first_x[0] = along_x(0, half, True)
+
+    get_ranks.wait()
+    get_panel.wait()
+    lanes = lax.broadcasted_iota(jnp.int32, (depth, rank), 1)
+
+    @pl.loop(0, n_tiles, unroll=4)
+    def _(t):
+        tile = mine[t].astype(F32)
+        tiles[row * n_tiles + t] = jnp.where(lanes < ranks[t], tile, jnp.zeros_like(tile)).astype(BF16)
+
+    get_pivots.wait()
+    for r in range(depth):
+        scale[pl.ds(r, 1), :] = jnp.full((1, rank), pivots[r], F32)
+
+    panel_in = own_row(tiles)
     panel_far = far_row(tiles, panel_in)
     far_x[0] = along_x_far(0, 0, in_x)
     far_z[0] = along_z_far(0, half, in_z)
+    some_z = along_z(1, 0, count=half // 2)
+    some_x = along_x(1, half, count=half // 2)
     get_left.wait()
     left_in = own_row(lefts)
     panel_last = last_row(tiles, panel_far)
+    get_pairs.wait()
     wait_all([panel_in[2], panel_far[1], panel_far[3], *panel_last])
 
-    @pl.loop(0, n_pairs, unroll=4)
-    def _(p):
-        to = lax.div(p, 2)
-        pr, tz, tx = lax.rem(p, 2), lax.div(to, SIDE), lax.rem(to, SIDE)
-        scaled = (tiles[pairs[0, p]].astype(F32) * scale[...]).astype(BF16)
-        ready[tx, tz, 0, pr] = scaled
-        ready[tx, tz, 1, pr] = tiles[pairs[1, p]]
-
-    own_transit = move(ready.at[x], transit.at[:, :, :, x])
-    stage_x = [
-        send(ready.at[wrap(x + d)], transit.at[:, :, :, x], at_col(0, d)) for d in (1, -1, 2)
-    ]
-
-    first_z[1] = along_z(1, 0)
-    first_x[1] = along_x(1, half)
+    @pl.loop(0, n_pairs // 2, unroll=2)
+    def _(to):
+        tz, tx = lax.div(to, SIDE), lax.rem(to, SIDE)
+        for pr, a, b in ((0, tx, tz), (1, tz, tx)):
+            left, right = pairs[0, 2 * to + pr], pairs[1, 2 * to + pr]
+            ready[pr, a, b, 0] = (tiles[left].astype(F32) * scale[...]).astype(BF16)
+            ready[pr, a, b, 1] = tiles[right]
+
+    place = (x, z)
+    step = (lambda d: at_col(0, d), lambda d: at_col(d, 0))
+    own_transit, operands_in = [], []
+    for pr in (0, 1):
+        me = transit.at[pr, :, :, place[pr]]
+        own_transit.append(move(ready.at[pr, place[pr]], me))
+        for d in (1, -1, 2):
+            operands_in.append(send(ready.at[pr, wrap(place[pr] + d)], me, step[pr](d)))
+
     late_z[0] = along_z_far(0, 0, first_z[0])
-
-    own_transit.wait()
-    wait_all(stage_x)
-    mid = pl.ds(z * SIDE, SIDE)
-    own_operands = move(transit.at[z], operands.at[:, :, mid])
-    stage_z = [
-        send(transit.at[wrap(z + d)], operands.at[:, :, mid], at_col(d, 0)) for d in (1, -1, 2)
-    ]
-
     late_x[0] = along_x_far(0, half, first_x[0])
+
+    for copy in own_transit:
+        copy.wait()
+    wait_all(operands_in)
+
+    def partial_sum(pr, at):
+        a = transit[pr, at, 0].reshape(SIDE * depth, rank)
+        b = transit[pr, at, 1].reshape(SIDE * depth, rank)
+        return lax.dot_general(a, b, (((0,), (0,)), ((), ())), preferred_element_type=F32)
+
+    partials_in = []
+    for pr in (0, 1):
+        at = place[1 - pr]
+        for d in (1, -1, 2):
+            there = wrap(at + d)
+            partial[pr, there] = partial_sum(pr, there).astype(BF16)
+            partials_in.append(send(partial.at[pr, there], arrived.at[pr, at], step[1 - pr](d)))
+
+    rest_z = along_z(1, half // 2, count=half // 2)
+    rest_x = along_x(1, half + half // 2, count=half // 2)
+    first_z[1] = [some_z[0], rest_z[1]]
+    first_x[1] = [some_x[0], rest_x[1]]
+    totals = [partial_sum(pr, place[1 - pr]) for pr in (0, 1)]
+    wait_all(partials_in)
+    for pr in (0, 1):
+        total = totals[pr]
+        for d in (1, 2, 3):
+            total = total + arrived[pr, wrap(place[1 - pr] + d)].astype(F32)
+        cores[z, x, pr] = total.astype(BF16)
+    core_in = []
+    for pr in (0, 1):
+        block = cores.at[z, x, pr]
+        core_in.append([send(block, block, step[pr](d)) for d in (1, -1, 2)])
+
+    first_z[-1] = along_z(-1, 0)
     first_x[-1] = along_x(-1, half)
-    first_z[-1] = along_z(-1, 0)
     left_far = far_row(lefts, left_in)
 
-    own_operands.wait()
-    wait_all(stage_z)
-    for pr in (0, 1):
-        a = operands[0, pr].reshape(SIDE * SIDE * depth, rank)
-        b = operands[1, pr].reshape(SIDE * SIDE * depth, rank)
-        total = lax.dot_general(a, b, (((0,), (0,)), ((), ())), preferred_element_type=F32)
-        cores[z, x, pr] = total.astype(BF16)
-    mine_0, mine_1 = cores.at[z, x, 0], cores.at[z, x, 1]
-    core_x = [send(mine_0, mine_0, at_col(0, d)) for d in (1, -1, 2)]
-    core_z = [send(mine_1, mine_1, at_col(d, 0)) for d in (1, -1, 2)]
+    def line(pr, d, first, count):
+        some = pl.ds(first, count)
+        if pr == 0:
+            return cores.at[wrap(z + d), some, 0]
+        return cores.at[some, wrap(x + d), 1]
+
+    line_in, line_far = [], []
+    for pr in (0, 1):
+        wait_all(core_in[pr])
+        block = line(pr, 0, 0, SIDE)
+        line_in.append([send(block, block, step[1 - pr](d)) for d in (1, -1)])
 
     wait_all(far_x[0] + far_z[0])
     first_z[2] = along_z(2, 0)
     first_x[2] = along_x(2, half)
     left_last = last_row(lefts, left_far)
-
-    wait_all(core_x)
-    line = cores.at[z, :, 0]
-    core_last = [send(line, line, at_col(d, 0)) for d in (1, -1, 2)]
-    wait_all(core_z)
-    line = cores.at[:, x, 1]
-    core_last += [send(line, line, at_col(0, d)) for d in (1, -1, 2)]
+    for pr in (0, 1):
+        for k, d in ((0, 1), (1, -1)):
+            line_in[pr][k].wait_recv()
+            block = line(pr, -d, k * SIDE // 2, SIDE // 2)
+            line_far.append(send(block, block, step[1 - pr](d)))
 
     for d in (-1, 1, 2):
         late_z[d] = along_z_far(d, 0, first_z[d])
         late_x[d] = along_x_far(d, half, first_x[d])
 
-    wait_all([left_in[2], left_far[1], left_far[3], *left_last, *core_last])
+    wait_all([left_in[2], left_far[1], left_far[3], *left_last, *line_far])
 
     @pl.loop(0, n_pairs, unroll=4)
     def _(p):
@@ -239,7 +269,7 @@
         group = whole[dz]
         columns = pl.ds(pl.multiple_of(wrap(z + dz) * width, width), width)
 
-        @pl.loop(0, n_pairs, unroll=8)
+        @pl.loop(0, n_pairs, unroll=16)
         def _(p):
             right = group[:, lax.rem(pairs[1, p], n_tiles)].reshape(width, rank)
             change = lax.dot_general(
@@ -249,6 +279,7 @@
 
     wait_all(late_x[0])
     update(0)
+    wait_all([some_x[1], rest_x[0], some_z[1], rest_z[0]])
     wait_all(late_x[1] + late_x[-1])
     update(1)
     update(-1)
@@ -281,14 +312,15 @@
             pltpu.VMEM((n_rows * n_tiles, part, rank), BF16),
             pltpu.VMEM((n_rows * n_tiles, depth, rank), BF16),
             pltpu.VMEM((n_tiles, depth, rank), BF16),
-            pltpu.VMEM((SIDE, SIDE, 2, 2, depth, rank), BF16),
-            pltpu.VMEM((SIDE, 2, 2, SIDE, depth, rank), BF16),
-            pltpu.VMEM((2, 2, SIDE * SIDE, depth, rank), BF16),
+            pltpu.VMEM((2, SIDE, SIDE, 2, depth, rank), BF16),
+            pltpu.VMEM((2, SIDE, 2, SIDE, depth, rank), BF16),
+            pltpu.VMEM((2, SIDE, rank, rank), BF16),
+            pltpu.VMEM((2, SIDE, rank, rank), BF16),
             pltpu.VMEM((SIDE, SIDE, 2, rank, rank), BF16),
             pltpu.VMEM((n_pairs, part, rank), BF16),
             pltpu.VMEM((depth, rank), F32),
-            pltpu.SemaphoreType.DMA((80,)),
-            pltpu.SemaphoreType.DMA((80,)),
+            pltpu.SemaphoreType.DMA((92,)),
+            pltpu.SemaphoreType.DMA((92,)),
             pltpu.SemaphoreType.DMA((12,)),
         ],
         compiler_params=pltpu.CompilerParams(

time: 70.2 us -> 66.6 us (0.949)
  the two profiles are of different devices: /device:TPU:1 before, /device:TPU:0 now
where the time goes in v3:
time: 66.6 us; the launch traced here: 66.5 us
  Pallas kernels  64.5 us (97%)
  local copies, waits for them, and re-layouts  2.02 us (3%)
    pallas_call x1, Pallas kernels, shards(): pl.pallas_call(kernel, out_shape=jax.ShapeDtypeStruct(targets.shape, targ...  64.5 us
    unnamed x1, local copies, waits for them, and re-layouts  2.02 us

profile of v3, /device:TPU:0, one launch (start us, length us, event | category | flops | bytes accessed | tf_op | source)
XLA Modules:
  0.0 66.5 jit_solution(6436900657131986276)
XLA Ops:
  0.0 64.5 %shard_map.64 = bf16[32,64,1024]{2,1,0:T(8,128)(2,1)S(1)} custom-call(bf16[32,32,128]{2,1,0:T(8,128)(2,1)} %panel.1, bf16[32,64,128]{2,1,0:T(8,128)(2,1)} %bases.1, f32[32]{0:T(128)} %pivot_list.1, s32[32]{0:T(128)} %rank_list.1, s32[2,32]{1,0:T(2,128)} %bitcast.1, bf16[32,64,1024]{2,1,0:T(8,128)(2,1)} %targets.1), custom_call_target="tpu_custom_call" | custom-call | tf_op jit(solution)/shard_map/pallas_call | solution.py:299
  64.5 2.0 %copy.8 = bf16[32,64,1024]{2,1,0:T(8,128)(2,1)} copy(bf16[32,64,1024]{2,1,0:T(8,128)(2,1)S(1)} %shard_map.64) | data formatting | bytes 8388608

commit v4 on v3

--- a/solution.py
+++ b/solution.py
@@ -111,25 +111,29 @@
         return [a, b]
 
     def own_row(array):
+        got = []
+        for k, d in ((0, 1), (1, -1), (1, 1), (0, -1)):
+            block = array.at[pl.ds(row * n_tiles + k * half, half)]
+            got.append(send(block, block, at_row(d)))
         block = array.at[own_tiles]
-        return [send(block, block, to) for to in (at_row(1), at_row(-1), twin)]
+        return got + [send(block, block, twin)]
 
     def far_row(array, arriving):
-        got = []
-        for k, d in ((0, -1), (1, 1)):
-            first = (wrap(y + d) * 2 + core) * n_tiles
-            arriving[k].wait_recv()
-            block = array.at[pl.ds(first + k * half, half)]
-            got.append(send(block, block, at_row(-d)))
-            block = array.at[pl.ds(first, n_tiles)]
-            got.append(send(block, block, twin))
-        return got
+        got, seen = [], []
+        for k, d in ((0, 1), (1, -1), (1, 1), (0, -1)):
+            first = (wrap(y - d) * 2 + core) * n_tiles + k * half
+            arriving[len(seen)].wait_recv()
+            block = array.at[pl.ds(first, half)]
+            seen.append(block)
+            if len(seen) <= 2:
+                got.append(send(block, block, at_row(d)))
+        return got + [send(block, block, twin) for block in seen]
 
     def last_row(array, arriving):
         first = (wrap(y + 2) * 2 + core) * n_tiles
         got = []
         for k in (0, 1):
-            arriving[2 * k].wait_recv()
+            arriving[k].wait_recv()
             block = array.at[pl.ds(first + k * half, half)]
             got.append(send(block, block, twin))
         return got
@@ -161,13 +165,11 @@
     panel_far = far_row(tiles, panel_in)
     far_x[0] = along_x_far(0, 0, in_x)
     far_z[0] = along_z_far(0, half, in_z)
-    some_z = along_z(1, 0, count=half // 2)
-    some_x = along_x(1, half, count=half // 2)
     get_left.wait()
     left_in = own_row(lefts)
     panel_last = last_row(tiles, panel_far)
     get_pairs.wait()
-    wait_all([panel_in[2], panel_far[1], panel_far[3], *panel_last])
+    wait_all([panel_in[4], *panel_far[2:], *panel_last])
 
     @pl.loop(0, n_pairs // 2, unroll=2)
     def _(to):
@@ -188,6 +190,8 @@
 
     late_z[0] = along_z_far(0, 0, first_z[0])
     late_x[0] = along_x_far(0, half, first_x[0])
+    some_z = along_z(1, 0, count=half // 2)
+    some_x = along_x(1, half, count=half // 2)
 
     for copy in own_transit:
         copy.wait()
@@ -252,7 +256,7 @@
         late_z[d] = along_z_far(d, 0, first_z[d])
         late_x[d] = along_x_far(d, half, first_x[d])
 
-    wait_all([left_in[2], left_far[1], left_far[3], *left_last, *line_far])
+    wait_all([left_in[4], *left_far[2:], *left_last, *line_far])
 
     @pl.loop(0, n_pairs, unroll=4)
     def _(p):
@@ -269,7 +273,7 @@
         group = whole[dz]
         columns = pl.ds(pl.multiple_of(wrap(z + dz) * width, width), width)
 
-        @pl.loop(0, n_pairs, unroll=16)
+        @pl.loop(0, n_pairs, unroll=32)
         def _(p):
             right = group[:, lax.rem(pairs[1, p], n_tiles)].reshape(width, rank)
             change = lax.dot_general(
@@ -319,8 +323,8 @@
             pltpu.VMEM((SIDE, SIDE, 2, rank, rank), BF16),
             pltpu.VMEM((n_pairs, part, rank), BF16),
             pltpu.VMEM((depth, rank), F32),
-            pltpu.SemaphoreType.DMA((92,)),
-            pltpu.SemaphoreType.DMA((92,)),
+            pltpu.SemaphoreType.DMA((100,)),
+            pltpu.SemaphoreType.DMA((100,)),
             pltpu.SemaphoreType.DMA((12,)),
         ],
         compiler_params=pltpu.CompilerParams(

time: 66.6 us -> 65.7 us (0.986)
  the two profiles are of different devices: /device:TPU:0 before, /device:TPU:1 now
where the time goes in v4:
time: 65.7 us; the launch traced here: 65.6 us
  Pallas kernels  63.6 us (97%)
  local copies, waits for them, and re-layouts  2.02 us (3%)
    pallas_call x1, Pallas kernels, shards(): pl.pallas_call(kernel, out_shape=jax.ShapeDtypeStruct(targets.shape, targ...  63.6 us
    unnamed x1, local copies, waits for them, and re-layouts  2.02 us

profile of v4, /device:TPU:1, one launch (start us, length us, event | category | flops | bytes accessed | tf_op | source)
XLA Modules:
  0.0 65.6 jit_solution(6659186909387384773)
XLA Ops:
  0.0 63.6 %shard_map.64 = bf16[32,64,1024]{2,1,0:T(8,128)(2,1)S(1)} custom-call(bf16[32,32,128]{2,1,0:T(8,128)(2,1)} %panel.1, bf16[32,64,128]{2,1,0:T(8,128)(2,1)} %bases.1, f32[32]{0:T(128)} %pivot_list.1, s32[32]{0:T(128)} %rank_list.1, s32[2,32]{1,0:T(2,128)} %bitcast.1, bf16[32,64,1024]{2,1,0:T(8,128)(2,1)} %targets.1), custom_call_target="tpu_custom_call" | custom-call | tf_op jit(solution)/shard_map/pallas_call | solution.py:303
  63.6 2.0 %copy.8 = bf16[32,64,1024]{2,1,0:T(8,128)(2,1)} copy(bf16[32,64,1024]{2,1,0:T(8,128)(2,1)S(1)} %shard_map.64) | data formatting | bytes 8388608

commit v5 on v4

--- a/solution.py
+++ b/solution.py
@@ -145,8 +145,6 @@
     far_x, far_z, first_z, first_x, late_z, late_x = {}, {}, {}, {}, {}, {}
     in_x = along_x(0, 0, True)
     in_z = along_z(0, half, True)
-    first_z[0] = along_z(0, 0, True)
-    first_x[0] = along_x(0, half, True)
 
     get_ranks.wait()
     get_panel.wait()
@@ -157,11 +155,13 @@
         tile = mine[t].astype(F32)
         tiles[row * n_tiles + t] = jnp.where(lanes < ranks[t], tile, jnp.zeros_like(tile)).astype(BF16)
 
+
+    panel_in = own_row(tiles)
+    first_z[0] = along_z(0, 0, True)
+    first_x[0] = along_x(0, half, True)
     get_pivots.wait()
     for r in range(depth):
         scale[pl.ds(r, 1), :] = jnp.full((1, rank), pivots[r], F32)
-
-    panel_in = own_row(tiles)
     panel_far = far_row(tiles, panel_in)
     far_x[0] = along_x_far(0, 0, in_x)
     far_z[0] = along_z_far(0, half, in_z)

time: 65.7 us -> 65.6 us (level)
  no operation moved by 1% of the time
where the time goes in v5:
time: 65.6 us; the launch traced here: 65.5 us
  Pallas kernels  63.5 us (97%)
  local copies, waits for them, and re-layouts  2.02 us (3%)
    pallas_call x1, Pallas kernels, shards(): pl.pallas_call(kernel, out_shape=jax.ShapeDtypeStruct(targets.shape, targ...  63.5 us
    unnamed x1, local copies, waits for them, and re-layouts  2.02 us

profile of v5, /device:TPU:1, one launch (start us, length us, event | category | flops | bytes accessed | tf_op | source)
XLA Modules:
  0.0 65.5 jit_solution(7718351885745659457)
XLA Ops:
  0.0 63.5 %shard_map.64 = bf16[32,64,1024]{2,1,0:T(8,128)(2,1)S(1)} custom-call(bf16[32,32,128]{2,1,0:T(8,128)(2,1)} %panel.1, bf16[32,64,128]{2,1,0:T(8,128)(2,1)} %bases.1, f32[32]{0:T(128)} %pivot_list.1, s32[32]{0:T(128)} %rank_list.1, s32[2,32]{1,0:T(2,128)} %bitcast.1, bf16[32,64,1024]{2,1,0:T(8,128)(2,1)} %targets.1), custom_call_target="tpu_custom_call" | custom-call | tf_op jit(solution)/shard_map/pallas_call | solution.py:303
  63.5 2.0 %copy.8 = bf16[32,64,1024]{2,1,0:T(8,128)(2,1)} copy(bf16[32,64,1024]{2,1,0:T(8,128)(2,1)S(1)} %shard_map.64) | data formatting | bytes 8388608
